TPU v7x, 512 devices: a whole 4x4x16 slice. The times are simulated.
512 devices in a mesh: ctx: 64 (over x_lo, z, core), tp: 8 (over y, x_hi).
Axes of the slice: x: 4 (x_hi: 2, x_lo: 2; x = x_hi * 2 + x_lo), y: 4, z: 16, core: 2. Of those that a mesh axis runs over, the one named last changes fastest.
Arguments:
- projected: bfloat16 [24576, 3, 8192], P('ctx', None, 'tp'), may hold values from -6 to 6
- dest_shard: int32 [24576], P('ctx'), may hold values from 0 to 63, as said below
- seg_start: int32 [24576], P('ctx'), may hold values from 0 to 24575, as said below
- short_filter: bfloat16 [7, 3, 8192], P(None, None, 'tp'), may hold values from -2 to 2
- long_filter: bfloat16 [128, 512], P(None, 'tp'), may hold values from -0.75 to 0.75
- long_decay: float32 [512], P('tp'), may hold values from 0.001953125 to 0.03125
- out_proj: bfloat16 [4096, 8192], P('ctx', 'tp'), may hold values from -0.0625 to 0.0625
Outputs:
- block_out: bfloat16 [24576, 4096], P('ctx', 'tp')
Inputs may be any that keep to these rules, and one draw needn't show every extreme that they name: `dest_shard`: every context shard is named by exactly 384 rows in all. In each aligned block of 384 rows (the rows of one loader shard) a shard is named by at most 12 rows, and the rows naming one shard are consecutive; every block names some shard exactly 12 times, and every shard is named exactly 12 times by some block. `seg_start`: Non-decreasing, at most the position itself, equal to the position where a genome begins; positions with equal values form one genome. The last packed position begins a genome of its own.
All inputs are finite; a program needn't handle non-finite values.
Results may differ from a plain program's by a relative error of at most 0.012.
Values may be sent and summed in bfloat16 or wider, within the bound.
A program may use at most 128 MiB of HBM per device.

v0:
```python
import jax
import jax.numpy as jnp
from jax import lax
from jax.sharding import PartitionSpec as P


def passed_along(block, axis, distance):
    devices = range(lax.axis_size(axis))
    route = [(i - distance, i) for i in devices if i - distance in devices]
    return lax.ppermute(block, axis, route)


def laid_out(pieces, dim):
    pieces = jnp.moveaxis(pieces, 0, dim)
    dims = pieces.shape
    return pieces.reshape(*dims[:dim], dims[dim] * dims[dim + 1], *dims[dim + 2 :])


def work_in_pieces(x, axis, dim, work, out_dim):
    width = x.shape[dim]
    pieces = jnp.split(x, 2, axis=dim) if width % 2 == 0 else [x]
    leading = jnp.arange(lax.axis_size(axis)) * width
    blocks = [lax.all_gather(piece, axis) for piece in pieces]
    made = [jax.vmap(work)(b, leading + k * (width // len(pieces))) for k, b in enumerate(blocks)]
    return laid_out(jnp.concatenate(made, axis=out_dim + 1), out_dim)


def cut_along(x, dim, size):
    before, after = (x.shape[:dim], x.shape[dim + 1 :])
    return jnp.moveaxis(x.reshape(*before, size, -1, *after), dim, 0)


def summed_on_arrival(x, axis, dim):
    size = lax.axis_size(axis)
    pieces = lax.all_to_all(cut_along(x, dim, size), axis, 0, 0, tiled=True)
    return jnp.sum(pieces.astype(jnp.float32), axis=0)


def short_conv(extended, weights, position, begins):
    short_len = weights.shape[0]
    out_rows = position.shape[0]
    summed = jnp.zeros((out_rows,) + extended.shape[1:], jnp.float32)
    for offset in range(short_len):
        allowed = position - offset >= begins
        product = (
            weights[offset].astype(jnp.float32)
            * extended[short_len - 1 - offset : short_len - 1 - offset + out_rows]
        )
        summed = summed + jnp.where(allowed[:, None, None], product, jnp.float32(0.0))
    return summed


def filter_conv(extended, tap_weights, position, begins):
    filter_len, filters = tap_weights.shape
    tok_rows = position.shape[0]
    channels = extended.shape[1]
    group_size = channels // filters
    channel_taps = jnp.repeat(tap_weights, group_size, axis=1)

    def add_tap(offset, running):
        shifted = lax.dynamic_slice_in_dim(extended, filter_len - offset, tok_rows, 0).astype(
            jnp.float32
        )
        tap_row = lax.dynamic_slice_in_dim(channel_taps, offset, 1, 0).astype(jnp.float32)
        allowed = position - offset >= begins
        return running + jnp.where(allowed[:, None], tap_row * shifted, jnp.float32(0.0))

    return lax.fori_loop(
        0, filter_len, add_tap, jnp.zeros((tok_rows, channels), jnp.float32), unroll=8
    )


def body(projected, dest_shard, seg_start, short_filter, long_filter, long_decay, out_proj):
    tok_rows = projected.shape[0]
    channels = projected.shape[2]
    shards = lax.axis_size("ctx")
    capacity = 2 * (tok_rows // shards)
    shard_ids = jnp.arange(shards)
    one_hot = (dest_shard[:, None] == shard_ids[None, :]).astype(jnp.int32)
    slot_rank = jnp.sum(one_hot * (jnp.cumsum(one_hot, axis=0) - 1), axis=1)
    counts = jnp.sum(one_hot, axis=0)
    slot_buffer = (
        jnp.zeros((shards * capacity, 3, channels), projected.dtype)
        .at[dest_shard * capacity + slot_rank]
        .set(projected)
    )
    received, got_counts = (
        lax.all_to_all(
            slot_buffer.reshape(shards, capacity, 3, channels),
            "ctx",
            split_axis=0,
            concat_axis=0,
            tiled=True,
        ),
        lax.all_to_all(counts, "ctx", split_axis=0, concat_axis=0, tiled=True),
    )
    ends_at = jnp.cumsum(got_counts)
    starts_at = ends_at - got_counts
    target = jnp.arange(tok_rows)
    source = jnp.sum((ends_at[None, :] <= target[:, None]).astype(jnp.int32), axis=1)
    source_start = jnp.sum(
        jnp.where(shard_ids[None, :] == source[:, None], starts_at[None, :], 0), axis=1
    )
    flat_index = (source * capacity + target - source_start).astype(jnp.int32)
    packed = jnp.take(received.reshape(shards * capacity, 3, channels), flat_index, axis=0)
    position = lax.axis_index("ctx") * tok_rows + target
    short_len = short_filter.shape[0]
    filter_len = long_filter.shape[0]
    front_rows = passed_along(packed[tok_rows - (short_len - 1) :], "ctx", 1)
    features = short_conv(
        jnp.concatenate([front_rows, packed], axis=0), short_filter, position, seg_start
    )
    key_value = (features[:, 1] * features[:, 2]).astype(jnp.bfloat16)
    rim_products = passed_along(key_value[tok_rows - (filter_len - 1) :], "ctx", 1)
    extended = jnp.concatenate(
        [jnp.zeros((1, channels), jnp.bfloat16), rim_products, key_value], axis=0
    )
    tap_index = jnp.arange(filter_len).astype(jnp.float32)
    tap_weights = (
        long_filter.astype(jnp.float32) * jnp.exp(-long_decay[None, :] * tap_index[:, None])
    ).astype(jnp.bfloat16)
    mixing = filter_conv(extended, tap_weights, position, seg_start)
    gated_out = (features[:, 0] * mixing).astype(jnp.bfloat16)
    contract = (((1,), (1,)), ((), ()))

    def project(weight_rows, first_row):
        return lax.dot_general(gated_out, weight_rows, contract, preferred_element_type=jnp.float32)

    partial_value = work_in_pieces(out_proj, "ctx", 0, project, 1)
    return summed_on_arrival(partial_value.astype(jnp.bfloat16), "tp", 1).astype(jnp.bfloat16)


def solution(mesh):
    placed = (
        P("ctx", None, "tp"),
        P("ctx"),
        P("ctx"),
        P(None, None, "tp"),
        P(None, "tp"),
        P("tp"),
        P("ctx", "tp"),
    )
    return jax.shard_map(
        body, mesh=mesh, in_specs=placed, out_specs=P("ctx", "tp"), check_vma=False
    )
```

profile of v0, /device:TPU:1, one launch (start us, length us, event | category | flops | bytes accessed | tf_op | source)
XLA Modules:
  0.0 589.5 jit_solution(13023633012028953816)
XLA Ops:
  10.0 18.1 %all-to-all-start = ((s32[64,1,1]{2,1,0:T(1,128)}), s32[64,1,1]{2,1,0:T(1,128)S(1)}, u32[]{:S(2)}, u32[]{:S(2)}) async-start(s32[64,1,1]{2,1,0:T(1,128)} %copy.50), calls=%async_computation | async-start | bytes 65536 | tf_op jit(solution)/shard_map/all_to_all | solution.py:95
  28.8 5.4 copy.53
  34.1 4.3 broadcast_in_dim.245
  38.4 50.0 %scatter_fusion = bf16[768,3,1024]{2,1,0:T(4,128)(2,1)} fusion(bf16[768,3,1024]{2,1,0:T(4,128)(2,1)} %broadcast_in_dim.245, s32[384]{0:T(512)S(1)} %compare_select_fusion.1, bf16[384,3,1024]{2,1,0:T(4,128)(2,1)} %copy.53), kind=kCustom, calls=%fused_computation.1 | custom fusion | bytes 7079424 | tf_op jit(solution)/shard_map/scatter | solution.py:85
  88.4 14.0 %all-to-all-start.1 = ((bf16[64,12,3,1024]{3,2,1,0:T(4,128)(2,1)}), bf16[64,12,3,1024]{3,2,1,0:T(4,128)(2,1)}, u32[]{:S(2)}, u32[]{:S(2)}) async-start(bf16[64,12,3,1024]{3,2,1,0:T(4,128)(2,1)} %bitcast.89), calls=%async_computation.1 | async-start | bytes 12582912 | tf_op jit(solution)/shard_map/all_to_all | solution.py:88
  105.7 300.7 %all-to-all-done.1 = bf16[64,12,3,1024]{3,2,1,0:T(4,128)(2,1)} async-done(((bf16[64,12,3,1024]{3,2,1,0:T(4,128)(2,1)}), bf16[64,12,3,1024]{3,2,1,0:T(4,128)(2,1)}, u32[]{:S(2)}, u32[]{:S(2)}) %all-to-all-start.1) | async-done | bytes 4718624 | tf_op jit(solution)/shard_map/all_to_all | solution.py:88
  406.4 7.8 %gather_fusion = bf16[384,3,1024]{2,1,0:T(4,128)(2,1)} fusion(bf16[768,3,1024]{2,1,0:T(4,128)(2,1)} %bitcast.5, s32[1024]{0:T(1024)S(1)} %pad_clamp_fusion), kind=kCustom, calls=%fused_computation | custom fusion | bytes 4720128 | tf_op jit(solution)/shard_map/jit(_take)/gather | solution.py:105
  421.3 17.1 %select_add_fusion.1 = f32[384,3,1024]{2,1,0:T(4,128)S(1)} fusion(bf16[384,3,1024]{2,1,0:T(4,128)(2,1)S(1)} %broadcast_select_fusion, bf16[6,3,1024]{2,1,0:T(4,128)(2,1)S(1)} %collective-permute-done, f32[3,1024]{1,0:T(4,128)S(1)} %get-tuple-element.385, f32[3,1024]{1,0:T(4,128)S(1)} %get-tuple-element.386, f32[3,1024]{1,0:T(4,128)S(1)} %get-tuple-element.387, ...), kind=kLoop, calls=%fused_computation.41 | loop fusion | flops 38928384 | bytes 7203456 | tf_op jit(solution)/shard_map/add | solution.py:49
  443.0 4.4 collective-permute-start.1
  451.9 69.2 %while.20 = (s32[]{:T(128)}, f32[384,1024]{1,0:T(8,128)S(1)}, s32[384]{0:T(512)S(1)}, bf16[128,1024]{1,0:T(8,128)(2,1)S(1)}, bf16[512,1024]{1,0:T(8,128)(2,1)S(1...) while((s32[]{:T(128)}, f32[384,1024]{1,0:T(8,128)S(1)}, ...), condition=%wide.region_9.10_spmd.clone.clone.clone, body=%wide.region_8.9_spmd.clone.clone.clone.clone.sunk | while | flops 12990915 | bytes 9527843 | solution.py:68
  452.1 4.1 fusion.61
  456.4 4.1 fusion.61
  460.7 4.1 fusion.61
  465.0 4.1 fusion.61
  469.4 4.1 fusion.61
  473.7 4.1 fusion.61
  478.0 4.1 fusion.61
  486.7 4.1 fusion.61
  491.0 4.1 fusion.61
  495.3 4.1 fusion.61
  499.7 4.1 fusion.61
  522.8 5.5 fusion.42
  528.4 5.5 fusion.45
  536.2 43.1 %all_to_all.22 = bf16[8,384,512]{1,2,0:T(8,128)(2,1)} all-to-all(bf16[8,384,512]{1,2,0:T(8,128)(2,1)S(1)} %bitcast.90), channel_id=1, replica_groups=mesh['ctx'=64,'tp'=8] {'tp'}, dimensions={0} | all-to-all | bytes 6291456 | tf_op jit(solution)/shard_map/all_to_all | solution.py:35
  (102 shorter events, 52.4 us)
Async XLA Ops:
  10.0 78.3 %all-to-all-start = ((s32[64,1,1]{2,1,0:T(1,128)}), s32[64,1,1]{2,1,0:T(1,128)S(1)}, u32[]{:S(2)}, u32[]{:S(2)}) async-start(s32[64,1,1]{2,1,0:T(1,128)} %copy.50), calls=%async_computation | async-start | bytes 65536 | tf_op jit(solution)/shard_map/all_to_all | solution.py:95
  88.4 14.0 %copy-start.2 = (bf16[64,1024]{1,0:T(8,128)(2,1)S(1)}, bf16[64,1024]{1,0:T(8,128)(2,1)}, u32[]{:S(2)}) copy-start(bf16[64,1024]{1,0:T(8,128)(2,1)} %param.15) | copy-start | bytes 393220
  88.4 15.5 %copy-start.1 = (bf16[7,3,1024]{2,0,1:T(8,128)(2,1)S(1)}, bf16[7,3,1024]{2,0,1:T(8,128)(2,1)}, u32[]{:S(2)}) copy-start(bf16[7,3,1024]{2,0,1:T(8,128)(2,1)} %param.12) | copy-start | bytes 129028
  88.4 318.0 %all-to-all-start.1 = ((bf16[64,12,3,1024]{3,2,1,0:T(4,128)(2,1)}), bf16[64,12,3,1024]{3,2,1,0:T(4,128)(2,1)}, u32[]{:S(2)}, u32[]{:S(2)}) async-start(bf16[64,12,3,1024]{3,2,1,0:T(4,128)(2,1)} %bitcast.89), calls=%async_computation.1 | async-start | bytes 12582912 | tf_op jit(solution)/shard_map/all_to_all | solution.py:88
  102.4 420.5 %all-gather.7.cloned.1.call-start = ((), (), s32[]{:S(2)}) async-start(), calls=%async_computation.4 | async-start | bytes 4259840 | tf_op jit(solution)/shard_map/all_gather | solution.py:23
  103.1 425.3 %all-gather.5.cloned.1.call-start = ((), (), s32[]{:S(2)}) async-start(), calls=%async_computation.3 | async-start | bytes 4259840 | tf_op jit(solution)/shard_map/all_gather | solution.py:23
  414.2 6.1 %copy-start.3 = (s32[384]{0:T(512)S(1)}, s32[384]{0:T(512)}, u32[]{:S(2)}) copy-start(s32[384]{0:T(512)} %param.11) | copy-start | bytes 4612
  418.1 3.1 collective-permute-start
  438.4 9.0 %copy-start.5 = (f32[64]{0:T(128)S(1)}, f32[64]{0:T(128)}, u32[]{:S(2)}) copy-start(f32[64]{0:T(128)} %param.14) | copy-start | bytes 772
  438.4 9.1 %copy-start.4 = (bf16[128,64]{0,1:T(8,128)(2,1)S(1)}, bf16[128,64]{0,1:T(8,128)(2,1)}, u32[]{:S(2)}) copy-start(bf16[128,64]{0,1:T(8,128)(2,1)} %param.13) | copy-start | bytes 49156
  442.4 5.0 copy-start
  443.0 8.6 %collective-permute-start.1 = (bf16[127,1024]{1,0:T(8,128)(2,1)S(1)}, bf16[127,1024]{1,0:T(8,128)(2,1)S(1)}, u32[]{:S(2)}, u32[]{:S(2)}) collective-permute-start(bf16[127,1024]{1,0:T(8,128)(2,1)S(1)} %bitcast.102), channel_id=1, source_target_pairs={{0,8},{8,16},{16,24},{24,32},{32,40},{40,48},{48,56},{56,64},{64,7... | collective-permute-start | bytes 780296 | tf_op jit(solution)/shard_map/ppermute | solution.py:10
Sparse Core Ops, SparseCore 0:
  105.3 219.1 all-gather.6
  326.7 145.4 all-gather.4
where the time goes:
time: 594 us; the launch traced here: 590 us
  waiting for transfers between devices  305 us (51%)
  other arithmetic  102 us (17%)
  local copies, waits for them, and re-layouts  74.3 us (13%)
  blocking collectives  43.1 us (7%)
  starting transfers between devices  38.6 us (6%)
  between operations  13.7 us (2%)
  matrix products  11.1 us (2%)
    all_to_all x1, waiting for transfers between devices, body(): lax.all_to_all(slot_buffer.reshape(shards, capacity, 3, channels), 'ctx',...  301 us
    add x16, other arithmetic, add_tap(): running + jnp.where(allowed[:, None], tap_row * shifted, jnp.float32(0.0))  65.8 us
    scatter x1, local copies, waits for them, and re-layouts, body(): slot_buffer = jnp.zeros((shards * capacity, 3, channels), projected.dtype...  50 us
    all_to_all x1, blocking collectives, summed_on_arrival(): pieces = lax.all_to_all(cut_along(x, dim, size), axis, 0, 0, tiled=True)  43.1 us
    all_to_all x1, starting transfers between devices, body(): lax.all_to_all(counts, 'ctx', split_axis=0, concat_axis=0, tiled=True)  18.1 us
    add x1, other arithmetic, short_conv(): summed + jnp.where(allowed[:, None, None], product, jnp.float32(0.0))  17.1 us
    all_to_all x1, starting transfers between devices, body(): lax.all_to_all(slot_buffer.reshape(shards, capacity, 3, channels), 'ctx',...  14 us
  transfers between devices with their start and end apart: 6, of which 3 were waited for; matrix products, arithmetic and copies ran while one was open for 29% of the time, Pallas kernels for 0%

commit v1 on v0

v1 whole, which is shorter than its diff:
```python
import functools

import jax
import jax.numpy as jnp
import numpy as np
from jax import lax
from jax.experimental import pallas as pl
from jax.experimental.pallas import tpu as pltpu
from jax.sharding import PartitionSpec as P

MESH = pl.DeviceIdType.MESH
BF = jnp.bfloat16
F32 = jnp.float32
I32 = jnp.int32

NZ = 16
NS = 4 * NZ
TOK = 384
CH = 1024
G = 4
CG = CH // G
W = 3 * CG
HALF = NZ // 2
PAIR = 12
HALO = 144
WORST = tuple(PAIR * (4 * (HALF - k) + 2) for k in range(1, HALF + 1))
LIMIT = 60 * 1024 * 1024


def up16(n):
    return -(-n // 16) * 16


def class_keys():
    d = np.arange(NS)
    zd, cd = (d // 2) % NZ, d % 2
    off = (zd[None, :] - np.arange(NZ)[:, None]) % NZ
    plus = (off > 0) & ((off < HALF) | ((off == HALF) & (cd[None, :] == 0)))
    kappa = np.where(off == 0, HALF, np.where(plus, HALF - off, HALF + NZ - off))
    return (kappa * NS + d[None, :]).astype(np.int32)


def column_starts(caps):
    total = sum(caps)
    offs = np.concatenate([[0], np.cumsum(caps)[:-1]])
    table = np.zeros((2, NZ), np.int32)
    for cm in range(2):
        for delta in range(1, NZ):
            if delta < HALF or (delta == HALF and cm == 0):
                table[cm, delta] = TOK + offs[delta - 1]
            else:
                k = NZ - delta
                table[cm, delta] = TOK + total + offs[k - 1] - (TOK - caps[k - 1])
    return table


def sort_kernel(pos_ref, proj_ref, out_ref):
    rows = lax.broadcasted_iota(I32, (TOK, TOK), 0)
    perm = (rows == pos_ref[...]).astype(F32).astype(BF)
    for i in range(3):
        out_ref[0, :, i * CG : (i + 1) * CG] = jnp.dot(
            perm, proj_ref[i], preferred_element_type=F32
        ).astype(BF)


def sort_rows(pos, proj):
    return pl.pallas_call(
        sort_kernel,
        grid=(G,),
        out_shape=jax.ShapeDtypeStruct((G, TOK, W), BF),
        in_specs=[
            pl.BlockSpec((1, TOK), lambda g: (0, 0)),
            pl.BlockSpec((3, TOK, CG), lambda g: (0, 0, g)),
        ],
        out_specs=pl.BlockSpec((1, TOK, W), lambda g: (g, 0, 0)),
        name="sort_rows",
    )(pos, proj)


def dispatch_kernel(
    caps,
    capm,
    sorted_ref,
    idx_ref,
    fin_ref,
    packed_ref,
    halo_ref,
    held,
    select,
    place,
    outgo,
    income,
    z_send,
    z_recv,
    m_send,
    m_recv,
    h_send,
    h_recv,
    own_sem,
):
    me = lax.axis_index("ctx")
    core = me % 2
    z = (me // 2) % NZ
    x = me // (2 * NZ)

    def at(xx, zz, cc):
        return {"ctx": (xx * NZ + zz) * 2 + cc}

    up, down = at(x, (z + 1) % NZ, core), at(x, (z + NZ - 1) % NZ, core)
    mates = [None, at(x, z, 1 - core), at(1 - x, z, core), at(1 - x, z, 1 - core)]
    after, before = {"ctx": (me + 1) % NS}, {"ctx": (me + NS - 1) % NS}

    barrier = pltpu.get_barrier_semaphore()
    greeted = [up, down] + mates[1:] + [after, before]
    for other in greeted:
        pl.semaphore_signal(barrier, inc=1, device_id=other, device_id_type=MESH)

    total = sum(caps)
    offs = [0]
    for cap in caps:
        offs.append(offs[-1] + cap)

    def own(g):
        return pltpu.make_async_copy(
            sorted_ref.at[g], held.at[g, pl.ds(0, TOK)], own_sem.at[g]
        )

    for g in range(G):
        own(g).start()

    pl.semaphore_wait(barrier, len(greeted))

    def hop(way, g, k):
        cap = caps[k - 1]
        if k == 1:
            src = sorted_ref.at[g, pl.ds(0 if way == 0 else TOK - cap, cap)]
        else:
            first = TOK + way * total + offs[k - 2]
            if way == 1:
                first = first + caps[k - 2] - cap
            src = held.at[g, pl.ds(first, cap)]
        return pltpu.make_async_remote_copy(
            src_ref=src,
            dst_ref=held.at[g, pl.ds(TOK + way * total + offs[k - 1], cap)],
            send_sem=z_send.at[way, g, k - 1],
            recv_sem=z_recv.at[way, g, k - 1],
            device_id=up if way == 0 else down,
            device_id_type=MESH,
        )

    def to_mate(g, r):
        return pltpu.make_async_remote_copy(
            src_ref=outgo.at[g, r - 1],
            dst_ref=income.at[g, pl.ds(r * capm, capm)],
            send_sem=m_send.at[g, r - 1],
            recv_sem=m_recv.at[g, r - 1],
            device_id=mates[r],
            device_id_type=MESH,
        )

    def to_next(g):
        return pltpu.make_async_remote_copy(
            src_ref=packed_ref.at[g, pl.ds(TOK - HALO, HALO)],
            dst_ref=halo_ref.at[g],
            send_sem=h_send.at[g],
            recv_sem=h_recv.at[g],
            device_id=after,
            device_id_type=MESH,
        )

    width = TOK + 2 * total

    def first_hops(g):
        for way in range(2):
            hop(way, g, 1).start()

    first_hops(0)
    for r in range(4):
        cols = lax.broadcasted_iota(I32, (capm, width), 1)
        select[r] = (cols == idx_ref[r]).astype(F32).astype(BF)
    cols = lax.broadcasted_iota(I32, (TOK, 4 * capm), 1)
    place[...] = (cols == fin_ref[...]).astype(F32).astype(BF)
    for g in range(G):
        own(g).wait()

    @pl.when(me == 0)
    def _():
        halo_ref[...] = jnp.zeros_like(halo_ref)

    order = (3, 2, 1, 0)

    def turn(t, carry):
        for j in range(4):

            @pl.when((t >= 1) & (t <= G))
            def _():
                for way in range(2):
                    hop(way, t - 1, j + 4).wait_recv()
                    hop(way, t - 1, j + 5).start()

            if j > 0:

                @pl.when(t < G)
                def _():
                    for way in range(2):
                        hop(way, t, j).wait_recv()
                        hop(way, t, j + 1).start()

            else:

                @pl.when((t >= 1) & (t < G))
                def _():
                    first_hops(t)

            @pl.when((t >= 2) & (t < G + 2))
            def _():
                g = t - 2
                if j == 0:
                    for way in range(2):
                        hop(way, g, 8).wait_recv()
                r = order[j]

                def tile(n, c):
                    lanes = pl.ds(pl.multiple_of(n * CG, CG), CG)
                    got = jnp.dot(
                        select[r], held[g, :, lanes], preferred_element_type=F32
                    ).astype(BF)
                    if r == 0:
                        income[g, 0:capm, lanes] = got
                    else:
                        outgo[g, r - 1, :, lanes] = got
                    return c

                lax.fori_loop(0, 3, tile, 0)
                if r > 0:
                    to_mate(g, r).start()

            if j == 1:

                @pl.when(t >= 3)
                def _():
                    g = t - 3
                    for r in range(1, 4):
                        to_mate(g, r).wait_recv()

                    def tile(n, c):
                        lanes = pl.ds(pl.multiple_of(n * CG, CG), CG)
                        packed_ref[g, :, lanes] = jnp.dot(
                            place[...], income[g, :, lanes], preferred_element_type=F32
                        ).astype(BF)
                        return c

                    lax.fori_loop(0, 3, tile, 0)

                    @pl.when(me < NS - 1)
                    def _():
                        to_next(g).start()

        return carry

    lax.fori_loop(0, G + 3, turn, 0)

    def finish(g, carry):
        for way in range(2):
            for k in range(1, HALF + 1):
                hop(way, g, k).wait_send()
        for r in range(1, 4):
            to_mate(g, r).wait_send()

        @pl.when(me < NS - 1)
        def _():
            to_next(g).wait_send()

        @pl.when(me > 0)
        def _():
            to_next(g).wait_recv()

        return carry

    lax.fori_loop(0, G, finish, 0)


def dispatch(caps, capm, collective, rows, idx, fin):
    width = TOK + 2 * sum(caps)
    vmem = pl.BlockSpec(memory_space=pltpu.VMEM)
    dma = pltpu.SemaphoreType.DMA
    return pl.pallas_call(
        functools.partial(dispatch_kernel, caps, capm),
        out_shape=(
            jax.ShapeDtypeStruct((G, TOK, W), BF),
            jax.ShapeDtypeStruct((G, HALO, W), BF),
        ),
        in_specs=[vmem] * 3,
        out_specs=(vmem, vmem),
        scratch_shapes=[
            pltpu.VMEM((G, width, W), BF),
            pltpu.VMEM((4, capm, width), BF),
            pltpu.VMEM((TOK, 4 * capm), BF),
            pltpu.VMEM((G, 3, capm, W), BF),
            pltpu.VMEM((G, 4 * capm, W), BF),
            dma((2, G, HALF)),
            dma((2, G, HALF)),
            dma((G, 3)),
            dma((G, 3)),
            dma((G,)),
            dma((G,)),
            dma((G,)),
        ],
        compiler_params=pltpu.CompilerParams(
            collective_id=collective, has_side_effects=True, vmem_limit_bytes=LIMIT
        ),
        name="dispatch",
    )(rows, idx, fin)


def filter_kernel(begin_ref, short_ref, long_ref, decay_ref, rows_ref, halo_ref, out_ref, ext, feat, kv, toep):
    shape = short_ref.shape
    taps_n = 128
    ext[0:HALO] = halo_ref[0].astype(F32)
    ext[HALO : HALO + TOK] = rows_ref[0].astype(F32)
    begin = begin_ref[...]

    groups = CG // 16
    tap = lax.broadcasted_iota(I32, (1, taps_n), 1).astype(F32)
    taps = (long_ref[...].astype(F32) * jnp.exp(-decay_ref[...] * tap)).astype(BF)
    back = (
        lax.broadcasted_iota(I32, (taps_n, 2 * taps_n), 1)
        == taps_n - lax.broadcasted_iota(I32, (taps_n, 2 * taps_n), 0)
    )
    turned = jnp.dot(taps, back.astype(F32).astype(BF), preferred_element_type=F32)

    block = 64
    for b in range(512 // block):
        first = b * block - 128
        local = lax.broadcasted_iota(I32, (block, 128), 0) + first
        if first < 0:
            start = jnp.broadcast_to(begin[0:1], (block, 128))
        else:
            start = jnp.broadcast_to(begin[first : first + block], (block, 128))
        age = local - start
        for n in range(CG // 128):
            made = []
            for i in range(3):
                if i == 0 and first < 0:
                    continue
                lanes = slice(i * CG + n * 128, i * CG + (n + 1) * 128)
                acc = None
                for j in range(shape[1]):
                    x = ext[HALO + first - j : HALO + first - j + block, lanes]
                    w = short_ref[i, j : j + 1, n * 128 : (n + 1) * 128].astype(F32)
                    term = jnp.where(age >= j, w * x, 0.0)
                    acc = term if acc is None else acc + term
                made.append(acc)
            kv[b * block : (b + 1) * block, n * 128 : (n + 1) * 128] = (
                made[-2] * made[-1]
            ).astype(BF)
            if first >= 0:
                feat[first : first + block, n * 128 : (n + 1) * 128] = made[0]

    for f in range(groups):
        band = jnp.broadcast_to(turned[f : f + 1], (128, 256))
        toep[f] = pltpu.roll(band, 0, 1, stride=1, stride_axis=0).astype(BF)
    lane_group = lax.broadcasted_iota(I32, (128, 128), 1) // 16
    for tb in range(TOK // 128):
        m = lax.broadcasted_iota(I32, (128, 256), 1) + (tb * 128 - 128)
        open_ = (m >= begin[tb * 128 : (tb + 1) * 128]).astype(F32).astype(BF)
        for n in range(CG // 128):
            cols = slice(n * 128, (n + 1) * 128)
            source = kv[tb * 128 : tb * 128 + 256, cols]
            mix = jnp.zeros((128, 128), F32)
            for f in range(8):
                part = jnp.dot(toep[n * 8 + f] * open_, source, preferred_element_type=F32)
                mix = jnp.where(lane_group == f, part, mix)
            out_ref[tb * 128 : (tb + 1) * 128, cols] = (
                feat[tb * 128 : (tb + 1) * 128, cols] * mix
            ).astype(BF)


def run_filters(begin, short, long_t, decay, rows, halo):
    groups = CG // 16
    return pl.pallas_call(
        filter_kernel,
        grid=(G,),
        out_shape=jax.ShapeDtypeStruct((TOK, CH), BF),
        in_specs=[
            pl.BlockSpec((TOK, 1), lambda g: (0, 0)),
            pl.BlockSpec((3, short.shape[1], CG), lambda g: (0, 0, g)),
            pl.BlockSpec((groups, 128), lambda g: (g, 0)),
            pl.BlockSpec((groups, 1), lambda g: (g, 0)),
            pl.BlockSpec((1, TOK, W), lambda g: (g, 0, 0)),
            pl.BlockSpec((1, HALO, W), lambda g: (g, 0, 0)),
        ],
        out_specs=pl.BlockSpec((TOK, CG), lambda g: (0, g)),
        scratch_shapes=[
            pltpu.VMEM((HALO + TOK, W), F32),
            pltpu.VMEM((TOK, CG), F32),
            pltpu.VMEM((512, CG), BF),
            pltpu.VMEM((groups, 128, 256), BF),
        ],
        name="filters",
    )(begin, short, long_t, decay, rows, halo)


def project_kernel(gated_ref, weight_ref, out_ref):
    out_ref[0] = lax.dot_general(
        gated_ref[...],
        weight_ref[...],
        (((1,), (1,)), ((), ())),
        preferred_element_type=F32,
    ).astype(BF)


def project(gated, weights, parts):
    wide = weights.shape[0] // parts
    return pl.pallas_call(
        project_kernel,
        grid=(parts,),
        out_shape=jax.ShapeDtypeStruct((parts, TOK, wide), BF),
        in_specs=[
            pl.BlockSpec((TOK, CH), lambda k: (0, 0)),
            pl.BlockSpec((wide, CH), lambda k: (k, 0)),
        ],
        out_specs=pl.BlockSpec((1, TOK, wide), lambda k: (k, 0, 0)),
        name="project",
    )(gated, weights)


def tables(dest, caps, capm):
    me = lax.axis_index("ctx")
    core, z, x = me % 2, (me // 2) % NZ, me // (2 * NZ)
    d = jnp.arange(NS)
    r = jnp.arange(TOK)
    hit = dest[:, None] == d[None, :]
    counts = jnp.sum(hit.astype(I32), axis=0)
    first = jnp.min(jnp.where(hit, r[:, None], TOK), axis=0)
    key = lax.dynamic_index_in_dim(jnp.asarray(class_keys()), z, 0, keepdims=False)
    base = jnp.sum(jnp.where(key[None, :] < key[:, None], counts[None, :], 0), axis=1)
    pos = r + jnp.sum(jnp.where(hit, (base - first)[None, :], 0), axis=1)
    table = lax.all_gather(jnp.concatenate([counts, base]), "ctx")
    return pos.astype(I32).reshape(1, TOK), table


def receive_tables(table, caps, capm):
    me = lax.axis_index("ctx")
    core, z, x = me % 2, (me // 2) % NZ, me // (2 * NZ)
    rel = jnp.arange(4)
    xm, cm = (x + rel // 2) % 2, (core + rel % 2) % 2
    dm = (xm * NZ + z) * 2 + cm
    column = table.reshape(2, NZ, 2, 2 * NS)
    column = lax.dynamic_index_in_dim(column, x, 0, keepdims=False)
    column = lax.dynamic_index_in_dim(column, core, 1, keepdims=False)
    pick = (dm[:, None] == jnp.arange(NS)[None, :]).astype(I32)
    cnt = jnp.sum(pick[:, None, :] * column[None, :, :NS], axis=2)
    base = jnp.sum(pick[:, None, :] * column[None, :, NS:], axis=2)
    zs = jnp.arange(NZ)
    delta = (z - zs) % NZ
    starts = jnp.asarray(column_starts(caps))
    by_delta = jnp.sum(
        jnp.where(delta[None, :, None] == zs[None, None, :], starts[:, None, :], 0), axis=2
    )
    start = jnp.where(cm[:, None] == 0, by_delta[0][None], by_delta[1][None]) + base
    lower = (zs[None, :] < zs[:, None]).astype(I32)
    cum = jnp.sum(cnt[:, None, :] * lower[None], axis=2)
    i = jnp.arange(capm)[None, :, None]
    live = (i >= cum[:, None, :]) & (i < (cum + cnt)[:, None, :])
    idx = jnp.sum(jnp.where(live, (start - cum)[:, None, :] + i + 1, 0), axis=2) - 1
    mine = jnp.sum(
        jnp.where(jnp.arange(NS)[None, :] == me, table[:, :NS], 0), axis=1
    )
    s = jnp.arange(NS)
    xs, zz, cs = s // (2 * NZ), (s // 2) % NZ, s % 2
    at = jnp.sum(jnp.where(s[None, :] < s[:, None], mine[None, :], 0), axis=1)
    same = (xs[None, :] == xs[:, None]) & (cs[None, :] == cs[:, None]) & (zz[None, :] < zz[:, None])
    within = jnp.sum(jnp.where(same, mine[None, :], 0), axis=1)
    rank = ((xs + x) % 2) * 2 + (cs + core) % 2
    p = jnp.arange(TOK)[:, None]
    live = (p >= at[None, :]) & (p < (at + mine)[None, :])
    fin = jnp.sum(jnp.where(live, (rank * capm + within - at)[None, :] + p, 0), axis=1)
    return idx.astype(I32).reshape(4, capm, 1), fin.astype(I32).reshape(TOK, 1)


def body(projected, dest_shard, seg_start, short_filter, long_filter, long_decay, out_proj):
    me = lax.axis_index("ctx")
    proj = jnp.transpose(projected, (1, 0, 2))
    caps = tuple(up16(c) for c in WORST)
    capm = PAIR * NZ
    pos, table = tables(dest_shard, caps, capm)
    rows = sort_rows(pos, proj)
    idx, fin = receive_tables(table, caps, capm)
    packed, halo = dispatch(caps, capm, 0, rows, idx, fin)
    begin = (seg_start - me * TOK).astype(I32).reshape(TOK, 1)
    gated = run_filters(
        begin,
        jnp.transpose(short_filter, (1, 0, 2)),
        jnp.transpose(long_filter, (1, 0)),
        long_decay.reshape(-1, 1),
        packed,
        halo,
    )
    weights = lax.all_gather(out_proj, "ctx", tiled=True)
    part = project(gated, weights, lax.axis_size("tp"))
    got = lax.all_to_all(part, "tp", 0, 0, tiled=True)
    return jnp.sum(got.astype(F32), axis=0).astype(BF)


def solution(mesh):
    placed = (
        P("ctx", None, "tp"),
        P("ctx"),
        P("ctx"),
        P(None, None, "tp"),
        P(None, "tp"),
        P("tp"),
        P("ctx", "tp"),
    )
    return jax.shard_map(
        body, mesh=mesh, in_specs=placed, out_specs=P("ctx", "tp"), check_vma=False
    )
```

time: 594 us -> 438 us (0.74)
  waiting for transfers between devices: 305 us -> 0.71 us
  Pallas kernels: 0 us -> 293 us
  other arithmetic: 102 us -> 6.39 us
  blocking collectives: 43.1 us -> 115 us
  local copies, waits for them, and re-layouts: 74.3 us -> 4.68 us
  starting transfers between devices: 38.6 us -> 0.01 us
  matrix products: 11.1 us -> 0 us
    all_to_all x2 -> x0, waiting for transfers between devices: 301 us -> none  [the longest x1 301 us: body(): lax.all_to_all(slot_buffer.reshape(shards, capacity, 3, channels), 'ctx',...]
    pallas_call x0 -> x4, Pallas kernels: none -> 293 us  [the longest x1 264 us: dispatch(): pl.pallas_call(functools.partial(dispatch_kernel, caps, capm), out_shape=...]
    add x17 -> x4, other arithmetic: 82.9 us -> 0.69 us  [the longest x1 0.58 us: tables(): pos = r + jnp.sum(jnp.where(hit, (base - first)[None, :], 0), axis=1)]
    all_gather x0 -> x1, blocking collectives: none -> 71 us  [tables(): table = lax.all_gather(jnp.concatenate([counts, base]), 'ctx')]
    scatter x1 -> x0, local copies, waits for them, and re-layouts: 50 us -> none  [body(): slot_buffer = jnp.zeros((shards * capacity, 3, channels), projected.dtype...]
    all_to_all x2 -> x0, starting transfers between devices: 32 us -> none  [the longest x1 18.1 us: body(): lax.all_to_all(counts, 'ctx', split_axis=0, concat_axis=0, tiled=True)]
    dot_general x2 -> x0, matrix products: 11.1 us -> none  [project(): lax.dot_general(gated_out, weight_rows, contract, preferred_element_type=...]
    gather x1 -> x0, local copies, waits for them, and re-layouts: 7.76 us -> none  [body(): jnp.take(received.reshape(shards * capacity, 3, channels), flat_index, ax...]
  transfers between devices with their start and end apart: 6 -> 1, of which waited for: 3 -> 0; matrix products, arithmetic and copies ran while one was open for 29% -> 2% of each run, Pallas kernels for 0% -> 65%
where the time goes in v1:
time: 438 us; the launch traced here: 434 us
  Pallas kernels  293 us (67%)
  blocking collectives  115 us (26%)
  between operations  13.5 us (3%)
  other arithmetic  6.39 us (1%)
  local copies, waits for them, and re-layouts  4.68 us (1%)
    pallas_call x1, Pallas kernels, dispatch(): pl.pallas_call(functools.partial(dispatch_kernel, caps, capm), out_shape=...  264 us
    all_gather x1, blocking collectives, tables(): table = lax.all_gather(jnp.concatenate([counts, base]), 'ctx')  71 us
    all_to_all x1, blocking collectives, body(): got = lax.all_to_all(part, 'tp', 0, 0, tiled=True)  44.1 us
    pallas_call x1, Pallas kernels, run_filters(): pl.pallas_call(filter_kernel, grid=(G,), out_shape=jax.ShapeDtypeStruct((...  15.3 us
    pallas_call x1, Pallas kernels, project(): pl.pallas_call(project_kernel, grid=(parts,), out_shape=jax.ShapeDtypeStr...  9.65 us
  transfers between devices with their start and end apart: 1, of which 0 were waited for; matrix products, arithmetic and copies ran while one was open for 2% of the time, Pallas kernels for 65%

profile of v1, /device:TPU:1, one launch (start us, length us, event | category | flops | bytes accessed | tf_op | source)
XLA Modules:
  0.0 433.7 jit_solution(12238475022689196842)
XLA Ops:
  6.5 0.7 all-gather.4.cloned.1.call-update
  7.3 0.7 dynamic-slice_bitcast_fusion
  8.0 0.8 select_reduce_fusion.2
  8.8 0.2 select_reduce_fusion.6
  9.1 71.0 %all-gather.1 = s32[64,1,128]{2,1,0:T(1,128)S(1)} all-gather(s32[1,1,128]{2,1,0:T(1,128)S(1)} %add_bitcast_fusion.1), channel_id=2, replica_groups=mesh['ctx'=64,'tp'=8] {'ctx'}, dimensions={0}, use_global_device_ids=true | all-gather | bytes 33280 | tf_op jit(solution)/shard_map/all_gather | solution.py:439
  80.3 0.8 select_reduce_fusion.7
  81.2 0.2 multiply_reduce_fusion
  81.4 0.2 multiply_reduce_fusion.1
  81.7 0.1 select_reduce_fusion.3
  81.8 0.9 copy.19.idx_ref
  82.9 0.2 select_reduce_fusion.4
  83.1 0.1 select_reduce_fusion
  83.2 0.8 reshape.364.fin_ref
  84.0 0.7 broadcast_subtract_fusion
  84.7 0.8 reshape.363.begin_ref
  85.5 1.4 copy.22.decay_ref
  86.9 0.8 select_reduce_fusion.1
  87.6 0.6 reshape_add_fusion.pos_ref
  88.2 4.8 %sort_rows.1.sorted_ref = bf16[4,384,768]{2,1,0:T(8,128)(2,1)} custom-call(s32[1,384]{1,0:T(1,128)} %reshape_add_fusion.pos_ref, bf16[3,384,1024]{2,1,0:T(8,128)(2,1)} %bitcast.17), custom_call_target="tpu_custom_call" | custom-call | tf_op jit(solution)/shard_map/sort_rows/pallas_call | solution.py:67
  93.0 263.5 %dispatch.1 = (bf16[4,384,768]{2,1,0:T(8,128)(2,1)}, bf16[4,144,768]{2,1,0:T(8,128)(2,1)}) custom-call(bf16[4,384,768]{2,1,0:T(8,128)(2,1)} %sort_rows.1.sorted_ref, s32[4,192,1]{2,1,0:T(8,128)} %copy.19.idx_ref, s32[384,1]{1,0:T(8,128)} %reshape.364.fin_ref), custom_call_target="tpu_custom_call" | custom-call | tf_op jit(solution)/shard_map/dispatch/pallas_call | solution.py:287
  356.5 15.3 %filters.1.gated_ref = bf16[384,1024]{1,0:T(8,128)(2,1)} custom-call(s32[384,1]{1,0:T(8,128)} %reshape.363.begin_ref, bf16[3,7,1024]{2,1,0:T(8,128)(2,1)} %bitcast.21, bf16[64,128]{1,0:T(8,128)(2,1)} %bitcast.22, f32[64,1]{1,0:T(8,128)} %copy.22.decay_ref, bf16[4,384,768]{2,1,0:T(8,128)(2,1)} %get-tuple-element.7.rows_ref, ...), custom_call_target="tpu_custom_call" | custom-call | tf_op jit(solution)/shard_map/filters/pallas_call | solution.py:381
  371.8 9.6 %project.1 = bf16[8,384,512]{2,1,0:T(8,128)(2,1)} custom-call(bf16[384,1024]{1,0:T(8,128)(2,1)} %filters.1.gated_ref, bf16[4096,1024]{1,0:T(8,128)(2,1)} %all-gather.4.cloned.1.call-done.weight_ref), custom_call_target="tpu_custom_call" | custom-call | tf_op jit(solution)/shard_map/project/pallas_call | solution.py:415
  381.5 44.1 %all_to_all.5 = bf16[8,384,512]{2,1,0:T(8,128)(2,1)S(1)} all-to-all(bf16[8,384,512]{2,1,0:T(8,128)(2,1)} %project.1), channel_id=1, replica_groups=mesh['ctx'=64,'tp'=8] {'tp'}, dimensions={0} | all-to-all | bytes 6291456 | tf_op jit(solution)/shard_map/all_to_all | solution.py:502
  425.6 1.3 reduce_sum.135
  (20 shorter events, 0.6 us)
Async XLA Ops:
  6.5 365.3 %all-gather.4.cloned.1.call-start = ((), (), s32[]{:S(2)}) async-start(), calls=%async_computation.1 | async-start | bytes 8519680 | tf_op jit(solution)/shard_map/all_gather | solution.py:500
Sparse Core Ops, SparseCore 0:
  9.5 138.5 all-gather.3
